TPU v7x, 32 devices: a whole 2x2x4 slice. The times are simulated.
32 devices in a mesh: band: 4 (over y, x), lon: 8 (over z, core).
Axes of the slice: x: 2, y: 2, z: 4, core: 2. Of those that a mesh axis runs over, the one named last changes fastest.
Arguments:
- atm_state: bfloat16 [2048, 64, 128], P(('band', 'lon')), may hold values from -6 to 6
- ocean_state: bfloat16 [4096, 64, 128], P(('band', 'lon')), may hold values from -6 to 6
- wet_mask: int32 [4096, 128], P(('band', 'lon')), may hold values 0 or 1
- remap_tiles: bfloat16 [32, 128, 128], replicated, may hold values from -0.5 to 0.5
- intersection_atm: int32 [32, 32, 2], P(('band', 'lon')), may hold values from 0 to 63
- intersection_ocean: int32 [32, 32, 2], P(('band', 'lon')), may hold values from 0 to 127
- intersection_tile: int32 [32, 32, 2], P(('band', 'lon')), may hold values from 0 to 31
- peer_count: int32 [32, 32], P(('band', 'lon')), may hold values from 0 to 2, as said below
- w_in: bfloat16 [256, 128], replicated, may hold values from -0.5 to 0.5
- w_mid: bfloat16 [2, 256, 256], replicated, may hold values from -0.375 to 0.375
- b_hidden: float32 [3, 256], replicated, may hold values from -3 to 3
- w_out: bfloat16 [16, 256], replicated, may hold values from -0.375 to 0.375
- b_out: float32 [16], replicated, may hold values from -3 to 3
- up_atm: float32 [64, 16], replicated, may hold values from -1.5 to 1.5
- up_ocean: float32 [64, 16], replicated, may hold values from -1.5 to 1.5
Outputs:
- atm_flux: float32 [2048, 16, 128], P(('band', 'lon'))
- ocean_flux: float32 [4096, 16, 128], P(('band', 'lon'))
Inputs may be any that keep to these rules, and one draw needn't show every extreme that they name: `peer_count`: A slot is live when its index is below the count. In every draw one owner receives 2 live slots from every device; a few devices have live slots to nearly every owner, the others to about a quarter.
All inputs are finite; a program needn't handle non-finite values. No bound on the sum of `wet_mask` on one device may be relied on, other than what follows from the above.
Results may differ from a plain program's by a relative error of at most 0.008.
Values may be sent and summed in bfloat16 or wider, within the bound.
A program may use at most 128 MiB of HBM per device.

v0:
```python
import jax
import jax.numpy as jnp
from jax import lax
from jax.sharding import PartitionSpec as P


def post_requests(wanted):
    return lax.all_to_all(wanted, ("band", "lon"), split_axis=0, concat_axis=0, tiled=True)


def send_blocks(outgoing):
    return lax.all_to_all(outgoing, ("band", "lon"), split_axis=0, concat_axis=0, tiled=True)


def send_back(outgoing):
    return lax.all_to_all(outgoing, ("band", "lon"), split_axis=0, concat_axis=0, tiled=True)


def send_forward(outgoing):
    return lax.all_to_all(outgoing, ("band", "lon"), split_axis=0, concat_axis=0, tiled=True)


def grouped_fluxes(
    arrived, ocean_blocks, tile_rows, wet_rows, remap_tiles, w_in, w_mid, b_hidden, w_out, b_out
):
    slot_total = arrived.shape[0]
    group_size = 64
    group_count = slot_total // group_size

    def regroup(values):
        return values.reshape((group_count, group_size) + values.shape[1:])

    def one_group(inputs):
        atm_group, ocean_group, tile_group, wet_group = inputs
        remap = remap_tiles[tile_group]
        on_ocean = jnp.einsum(
            "sca,sab->scb", atm_group, remap, preferred_element_type=jnp.float32
        ).astype(jnp.bfloat16)
        hidden = jnp.concatenate([on_ocean, ocean_group], axis=1)
        hidden = jax.nn.silu(
            jnp.einsum("hk,skb->shb", w_in, hidden, preferred_element_type=jnp.float32)
            + b_hidden[0][None, :, None]
        ).astype(jnp.bfloat16)
        for level_index in range(w_mid.shape[0]):
            hidden = jax.nn.silu(
                jnp.einsum(
                    "hk,skb->shb", w_mid[level_index], hidden, preferred_element_type=jnp.float32
                )
                + b_hidden[level_index + 1][None, :, None]
            ).astype(jnp.bfloat16)
        fluxes = (
            (
                jnp.einsum("fh,shb->sfb", w_out, hidden, preferred_element_type=jnp.float32)
                + b_out[None, :, None]
            )
            * wet_group[:, None, :]
        ).astype(jnp.bfloat16)
        back = jnp.einsum("sfb,sab->sfa", fluxes, remap, preferred_element_type=jnp.float32)
        return (fluxes, back)

    fluxes, back = lax.map(
        one_group, (regroup(arrived), regroup(ocean_blocks), regroup(tile_rows), regroup(wet_rows))
    )
    return (
        fluxes.reshape((slot_total,) + fluxes.shape[2:]),
        back.reshape((slot_total,) + back.shape[2:]),
    )


def local(
    atm_state,
    ocean_state,
    wet_mask,
    remap_tiles,
    intersection_atm,
    intersection_ocean,
    intersection_tile,
    peer_count,
    w_in,
    w_mid,
    b_hidden,
    w_out,
    b_out,
    up_atm,
    up_ocean,
):
    band_count = lax.axis_size("band")
    lon_count = lax.axis_size("lon")
    peer_total = band_count * lon_count
    peer_slots = intersection_atm.shape[2]
    slot_total = peer_total * peer_slots
    served = post_requests(intersection_atm[0]).reshape(slot_total)
    ocean_rows = intersection_ocean[0].reshape(slot_total)
    tile_rows = intersection_tile[0].reshape(slot_total)
    live_mask = (jnp.arange(peer_slots, dtype=jnp.int32)[None, :] < peer_count[0][:, None]).reshape(
        slot_total
    )
    wet_float = wet_mask.astype(jnp.float32)
    wet_rows = wet_float[ocean_rows] * live_mask.astype(jnp.float32)[:, None]
    ocean_now = ocean_state
    first_arrived = None
    next_arrived = None
    atm_flux = None
    ocean_flux = None
    for substep in range(2):
        if substep == 1:
            arrived = next_arrived
        else:
            outgoing = atm_state[served].reshape((peer_total, peer_slots) + atm_state.shape[1:])
            arrived = send_blocks(outgoing).reshape((slot_total,) + atm_state.shape[1:])
        if substep == 0:
            first_arrived = arrived
        fluxes, back = grouped_fluxes(
            arrived,
            ocean_now[ocean_rows],
            tile_rows,
            wet_rows,
            remap_tiles,
            w_in,
            w_mid,
            b_hidden,
            w_out,
            b_out,
        )
        ocean_flux = (
            jnp.zeros((ocean_state.shape[0],) + fluxes.shape[1:], jnp.float32)
            .at[ocean_rows]
            .add(fluxes.astype(jnp.float32))
        )
        returned = send_back(back.reshape((peer_total, peer_slots) + back.shape[1:])).reshape(
            (slot_total,) + back.shape[1:]
        )
        atm_flux = (
            jnp.zeros((atm_state.shape[0],) + back.shape[1:], jnp.float32).at[served].add(returned)
        )
        if substep == 0:
            ocean_now = (
                ocean_state.astype(jnp.float32)
                + wet_float[:, None, :]
                * jnp.einsum("cf,nfb->ncb", up_ocean, ocean_flux, precision=lax.Precision.HIGHEST)
            ).astype(jnp.bfloat16)
            forward_out = atm_flux[served].reshape((peer_total, peer_slots) + atm_flux.shape[1:])
            forwarded = send_forward(forward_out).reshape((slot_total,) + atm_flux.shape[1:])
            next_arrived = (
                first_arrived.astype(jnp.float32)
                + jnp.einsum("cf,nfa->nca", up_atm, forwarded, precision=lax.Precision.HIGHEST)
            ).astype(jnp.bfloat16)
    return (atm_flux, ocean_flux)


def solution(mesh):
    placed = (
        P(("band", "lon"), None, None),
        P(("band", "lon"), None, None),
        P(("band", "lon"), None),
        P(),
        P(("band", "lon"), None, None),
        P(("band", "lon"), None, None),
        P(("band", "lon"), None, None),
        P(("band", "lon"), None),
        P(),
        P(),
        P(),
        P(),
        P(),
        P(),
        P(),
    )
    return jax.shard_map(
        local,
        mesh=mesh,
        in_specs=placed,
        out_specs=(P(("band", "lon"), None, None), P(("band", "lon"), None, None)),
        check_vma=False,
    )
```

profile of v0, /device:TPU:0, one launch (start us, length us, event | category | flops | bytes accessed | tf_op | source)
XLA Modules:
  0.0 170.4 jit_solution(6667536879505175853)
XLA Ops:
  0.6 0.0 copy-start
  0.7 0.0 copy-start.6
  0.7 0.8 copy.29
  1.5 14.3 %all_to_all.29 = s32[32,1,2]{2,1,0:T(1,128)S(1)} all-to-all(s32[32,1,2]{2,1,0:T(1,128)S(1)} %copy.29), channel_id=1, replica_groups=mesh['band'=4,'lon'=8] {'band','lon'}, dimensions={0} | all-to-all | bytes 512 | tf_op jit(solution)/shard_map/all_to_all | solution.py:8
  15.8 0.5 broadcast.127
  16.3 0.7 reduce.3
  17.0 0.1 reshape.158
  17.1 2.9 %gather_fusion = bf16[64,64,128]{2,1,0:T(8,128)(2,1)} fusion(bf16[64,64,128]{2,1,0:T(8,128)(2,1)} %param.15, s32[1024]{0:T(1024)S(1)} %pad_clamp_fusion.2), kind=kCustom, calls=%fused_computation | custom fusion | bytes 2097408 | tf_op jit(solution)/shard_map/gather | solution.py:109
  20.0 3.4 %all-to-all-start.1 = ((bf16[32,2,64,128]{3,2,1,0:T(8,128)(2,1)}), bf16[32,2,64,128]{3,2,1,0:T(8,128)(2,1)}, u32[]{:S(2)}, u32[]{:S(2)}) async-start(bf16[32,2,64,128]{3,2,1,0:T(8,128)(2,1)} %bitcast.2), calls=%async_computation.1 | async-start | bytes 2097152 | tf_op jit(solution)/shard_map/all_to_all | solution.py:12
  23.4 0.8 copy.30
  24.2 0.1 squeeze.46
  24.3 0.8 copy.31
  25.1 0.1 reshape_squeeze.3
  25.2 0.8 convert_element_type.84
  26.0 3.2 %gather_fusion.2 = bf16[64,64,128]{2,1,0:T(8,128)(2,1)} fusion(bf16[128,64,128]{2,1,0:T(8,128)(2,1)} %param.16, s32[1024]{0:T(1024)S(1)} %pad_clamp_fusion), kind=kCustom, calls=%fused_computation.2 | custom fusion | bytes 2097408 | tf_op jit(solution)/shard_map/gather | solution.py:115
  29.3 0.6 gather_fusion.3
  29.9 0.7 fusion.108
  30.6 0.1 reshape.165
  30.7 1.0 gather_fusion.1
  31.7 0.1 broadcast_multiply_fusion
  31.8 19.1 %all-to-all-done.1 = bf16[32,2,64,128]{3,2,1,0:T(8,128)(2,1)} async-done(((bf16[32,2,64,128]{3,2,1,0:T(8,128)(2,1)}), bf16[32,2,64,128]{3,2,1,0:T(8,128)(2,1)}, u32[]{:S(2)}, u32[]{:S(2)}) %all-to-all-start.1) | async-done | bytes 1048608 | tf_op jit(solution)/shard_map/all_to_all | solution.py:12
  50.9 2.9 %convolution_convert_fusion.1 = bf16[64,64,128]{2,1,0:T(8,128)(2,1)} fusion(bf16[64,64,128]{2,1,0:T(8,128)(2,1)} %bitcast.3, bf16[64,128,128]{2,1,0:T(8,128)(2,1)S(1)} %gather_fusion.1), kind=kOutput, calls=%fused_computation.65 | convolution fusion | flops 134742016 | bytes 4194304 | tf_op jit(solution)/shard_map/while/body/eval_jaxpr/sca,sab->scb/dot_general | solution.py:36
  53.7 7.4 %fusion.31 = f32[64,128,256]{2,1,0:T(8,128)} fusion(f32[256]{0:T(256)S(1)} %bitcast.199, bf16[64,64,128]{2,1,0:T(8,128)(2,1)} %gather_fusion.2, bf16[64,64,128]{2,1,0:T(8,128)(2,1)} %convolution_convert_fusion.1, bf16[2,256,256]{2,1,0:T(8,128)(2,1)} %param.24, bf16[256,128]{1,0:T(8,128)(2,1)S(1)} %copy-done.6), kind=kOutput, calls=%fused_computation.51 | convolution fusion | flops 1627389952 | bytes 10683392 | tf_op jit(solution)/shard_map/while/body/eval_jaxpr/hk,skb->shb/dot_general | solution.py:46
  61.1 6.9 %fusion.87 = bf16[64,128,16]{1,2,0:T(8,128)(2,1)S(1)} fusion(f32[256]{0:T(256)S(1)} %bitcast.197, f32[64,128,256]{2,1,0:T(8,128)} %fusion.31, f32[256]{0:T(256)S(1)} %bitcast.195, f32[64,128]{1,0:T(8,128)S(1)} %broadcast_multiply_fusion, f32[16]{0:T(128)S(1)} %copy-done.9, bf16[2,256,256]{2,1,0:T(8,128)(2,1)} %param.24, bf16[16,256]{1,0:T(8,128)(2,1)S(1)} %copy-done.8), kind=kOutput, calls=%fused_computation.71 | convolution fusion | flops 1166409728 | bytes 8824896 | tf_op jit(solution)/shard_map/while/body/eval_jaxpr/fh,shb->sfb/dot_general | solution.py:53
  68.0 1.2 fusion.127
  69.2 18.6 %all_to_all.30 = f32[32,2,16,128]{3,2,1,0:T(8,128)} all-to-all(f32[32,2,16,128]{3,2,1,0:T(8,128)S(1)} %bitcast.193), channel_id=1, replica_groups=mesh['band'=4,'lon'=8] {'band','lon'}, dimensions={0} | all-to-all | bytes 1048576 | tf_op jit(solution)/shard_map/all_to_all | solution.py:16
  87.8 0.8 broadcast.94.clone
  88.7 8.4 %scatter_fusion = f32[64,16,128]{2,1,0:T(8,128)} fusion(f32[64,16,128]{2,1,0:T(8,128)} %broadcast.94.clone, s32[64]{0:T(128)S(1)} %fusion.113, f32[64,16,128]{2,1,0:T(8,128)} %bitcast.191), kind=kCustom, calls=%fused_computation.6 | custom fusion | flops 131072 | bytes 1573120 | tf_op jit(solution)/shard_map/scatter-add | solution.py:134
  97.0 2.4 %gather_fusion.4 = f32[64,16,128]{2,1,0:T(8,128)} fusion(f32[64,16,128]{2,1,0:T(8,128)} %scatter_fusion, s32[1024]{0:T(1024)S(1)} %pad_clamp_fusion.2), kind=kCustom, calls=%fused_computation.4 | custom fusion | bytes 1048832 | tf_op jit(solution)/shard_map/gather | solution.py:142
  99.5 3.5 %all-to-all-start.3 = ((f32[32,2,16,128]{3,2,1,0:T(8,128)}), f32[32,2,16,128]{3,2,1,0:T(8,128)}, u32[]{:S(2)}, u32[]{:S(2)}) async-start(f32[32,2,16,128]{3,2,1,0:T(8,128)} %bitcast.190), calls=%async_computation.3 | async-start | bytes 1048576 | tf_op jit(solution)/shard_map/all_to_all | solution.py:20
  103.0 0.8 convert_bitcast_fusion.1
  103.8 1.0 broadcast.99.clone
  104.9 8.4 %scatter_fusion.1 = f32[128,16,128]{2,1,0:T(8,128)} fusion(f32[128,16,128]{2,1,0:T(8,128)} %broadcast.99.clone, s32[64]{0:T(128)S(1)} %fusion.115, f32[64,16,128]{2,1,0:T(8,128)} %convert_bitcast_fusion.1), kind=kCustom, calls=%fused_computation.7 | custom fusion | flops 131072 | bytes 1573120 | tf_op jit(solution)/shard_map/scatter-add | solution.py:128
  113.2 7.1 %fusion.24 = bf16[128,64,128]{2,1,0:T(8,128)(2,1)} fusion(bf16[128,64,128]{2,1,0:T(8,128)(2,1)} %param.16, f32[128,16,128]{2,1,0:T(8,128)} %scatter_fusion.1, f32[128,128]{1,0:T(8,128)S(1)} %convert_element_type.84, f32[64,16]{0,1:T(8,128)S(1)} %copy-done.3), kind=kOutput, calls=%fused_computation.47 | convolution fusion | flops 205520896 | bytes 5312512 | tf_op jit(solution)/shard_map/cf,nfb->ncb/dot_general | solution.py:140
  120.3 3.2 %gather_fusion.5 = bf16[64,64,128]{2,1,0:T(8,128)(2,1)} fusion(bf16[128,64,128]{2,1,0:T(8,128)(2,1)} %fusion.24, s32[1024]{0:T(1024)S(1)} %pad_clamp_fusion), kind=kCustom, calls=%fused_computation.5 | custom fusion | bytes 2097408 | tf_op jit(solution)/shard_map/gather | solution.py:115
  123.5 3.3 %fusion.53 = bf16[64,64,128]{2,1,0:T(8,128)(2,1)S(1)} fusion(bf16[64,64,128]{2,1,0:T(8,128)(2,1)} %bitcast.3, f32[64,16,128]{2,1,0:T(8,128)} %bitcast.22, f32[64,16]{0,1:T(8,128)S(1)} %copy-done.4), kind=kOutput, calls=%fused_computation.63 | convolution fusion | flops 102236160 | bytes 2625536 | tf_op jit(solution)/shard_map/cf,nfa->nca/dot_general | solution.py:146
  126.8 1.8 %convolution_convert_fusion = bf16[64,64,128]{2,1,0:T(8,128)(2,1)} fusion(bf16[64,64,128]{2,1,0:T(8,128)(2,1)S(1)} %fusion.53, bf16[64,128,128]{2,1,0:T(8,128)(2,1)S(1)} %gather_fusion.1), kind=kOutput, calls=%fused_computation.64 | convolution fusion | flops 134742016 | bytes 4194304 | tf_op jit(solution)/shard_map/while/body/eval_jaxpr/sca,sab->scb/dot_general | solution.py:36
  128.6 7.4 %fusion.27 = f32[64,128,256]{2,1,0:T(8,128)} fusion(f32[256]{0:T(256)S(1)} %bitcast.200, bf16[64,64,128]{2,1,0:T(8,128)(2,1)} %gather_fusion.5, bf16[64,64,128]{2,1,0:T(8,128)(2,1)} %convolution_convert_fusion, bf16[2,256,256]{2,1,0:T(8,128)(2,1)} %param.24, bf16[256,128]{1,0:T(8,128)(2,1)S(1)} %copy-done.7), kind=kOutput, calls=%fused_computation.49 | convolution fusion | flops 1627389952 | bytes 10683392 | tf_op jit(solution)/shard_map/while/body/eval_jaxpr/hk,skb->shb/dot_general | solution.py:46
  135.9 6.9 %fusion.82 = bf16[64,128,16]{1,2,0:T(8,128)(2,1)S(1)} fusion(f32[256]{0:T(256)S(1)} %bitcast.198, f32[64,128,256]{2,1,0:T(8,128)} %fusion.27, f32[256]{0:T(256)S(1)} %bitcast.196, f32[64,128]{1,0:T(8,128)S(1)} %broadcast_multiply_fusion, f32[16]{0:T(128)S(1)} %copy-done.9, bf16[2,256,256]{2,1,0:T(8,128)(2,1)} %param.24, bf16[16,256]{1,0:T(8,128)(2,1)S(1)} %copy-done.8), kind=kOutput, calls=%fused_computation.70 | convolution fusion | flops 1166409728 | bytes 8824896 | tf_op jit(solution)/shard_map/while/body/eval_jaxpr/fh,shb->sfb/dot_general | solution.py:53
  142.8 2.0 %fusion.128 = f32[64,16,128]{2,1,0:T(8,128)} fusion(bf16[64,128,16]{1,2,0:T(8,128)(2,1)S(1)} %fusion.82, bf16[64,128,128]{2,1,0:T(8,128)(2,1)S(1)} %gather_fusion.1), kind=kOutput, calls=%fused_computation.108 | convolution fusion | flops 33554432 | bytes 2883584 | tf_op jit(solution)/shard_map/while/body/eval_jaxpr/sfb,sab->sfa/dot_general | solution.py:58
  144.8 5.6 %all-to-all-start.4 = ((f32[32,2,16,128]{3,2,1,0:T(8,128)}), f32[32,2,16,128]{3,2,1,0:T(8,128)S(1)}, u32[]{:S(2)}, u32[]{:S(2)}) async-start(f32[32,2,16,128]{3,2,1,0:T(8,128)} %bitcast.192), calls=%async_computation.4 | async-start | bytes 1048576 | tf_op jit(solution)/shard_map/all_to_all | solution.py:16
  150.5 0.1 broadcast.99
  150.5 2.9 %scatter_fusion.3 = f32[128,16,128]{2,1,0:T(8,128)S(1)} fusion(f32[128,16,128]{2,1,0:T(8,128)S(1)} %broadcast.99, s32[64]{0:T(128)S(1)} %fusion.115, f32[64,16,128]{2,1,0:T(8,128)S(1)} %convert_bitcast_fusion), kind=kCustom, calls=%fused_computation.9 | custom fusion | flops 131072 | bytes 1573120 | tf_op jit(solution)/shard_map/scatter-add | solution.py:128
  153.4 0.0 copy-start.1
  153.4 13.2 %all-to-all-done.4 = f32[32,2,16,128]{3,2,1,0:T(8,128)S(1)} async-done(((f32[32,2,16,128]{3,2,1,0:T(8,128)}), f32[32,2,16,128]{3,2,1,0:T(8,128)S(1)}, u32[]{:S(2)}, u32[]{:S(2)}) %all-to-all-start.4) | async-done | bytes 524320 | tf_op jit(solution)/shard_map/all_to_all | solution.py:16
  166.7 2.9 %scatter_fusion.2 = f32[64,16,128]{2,1,0:T(8,128)S(1)} fusion(f32[64,16,128]{2,1,0:T(8,128)S(1)} %broadcast.94, s32[64]{0:T(128)S(1)} %fusion.113, f32[64,16,128]{2,1,0:T(8,128)S(1)} %bitcast.189), kind=kCustom, calls=%fused_computation.8 | custom fusion | flops 131072 | bytes 1573120 | tf_op jit(solution)/shard_map/scatter-add | solution.py:134
  169.6 0.0 copy-start.2
  169.6 0.8 copy-done.2
  (25 shorter events, 0.1 us)
Async XLA Ops:
  0.6 30.1 %copy-start = (bf16[32,128,128]{2,1,0:T(8,128)(2,1)S(1)}, bf16[32,128,128]{2,1,0:T(8,128)(2,1)}, u32[]{:S(2)}) copy-start(bf16[32,128,128]{2,1,0:T(8,128)(2,1)} %param.18) | copy-start | bytes 3145732
  0.6 31.1 %copy-start.5 = (f32[3,256]{1,0:T(4,128)S(1)}, f32[3,256]{1,0:T(4,128)}, u32[]{:S(2)}) copy-start(f32[3,256]{1,0:T(4,128)} %param.25) | copy-start | bytes 9220
  0.7 53.1 %copy-start.6 = (bf16[256,128]{1,0:T(8,128)(2,1)S(1)}, bf16[256,128]{1,0:T(8,128)(2,1)}, u32[]{:S(2)}) copy-start(bf16[256,128]{1,0:T(8,128)(2,1)} %param.23) | copy-start | bytes 196612
  20.0 30.8 %all-to-all-start.1 = ((bf16[32,2,64,128]{3,2,1,0:T(8,128)(2,1)}), bf16[32,2,64,128]{3,2,1,0:T(8,128)(2,1)}, u32[]{:S(2)}, u32[]{:S(2)}) async-start(bf16[32,2,64,128]{3,2,1,0:T(8,128)(2,1)} %bitcast.2), calls=%async_computation.1 | async-start | bytes 2097152 | tf_op jit(solution)/shard_map/all_to_all | solution.py:12
  53.7 7.4 %copy-start.8 = (bf16[16,256]{1,0:T(8,128)(2,1)S(1)}, bf16[16,256]{1,0:T(8,128)(2,1)}, u32[]{:S(2)}) copy-start(bf16[16,256]{1,0:T(8,128)(2,1)} %param.26) | copy-start | bytes 24580
  53.7 7.4 %copy-start.9 = (f32[16]{0:T(128)S(1)}, f32[16]{0:T(128)}, u32[]{:S(2)}) copy-start(f32[16]{0:T(128)} %param.27) | copy-start | bytes 196
  97.0 16.2 %copy-start.3 = (f32[64,16]{0,1:T(8,128)S(1)}, f32[64,16]{0,1:T(8,128)}, u32[]{:S(2)}) copy-start(f32[64,16]{0,1:T(8,128)} %param.29) | copy-start | bytes 12292
  99.5 24.1 %all-to-all-start.3 = ((f32[32,2,16,128]{3,2,1,0:T(8,128)}), f32[32,2,16,128]{3,2,1,0:T(8,128)}, u32[]{:S(2)}, u32[]{:S(2)}) async-start(f32[32,2,16,128]{3,2,1,0:T(8,128)} %bitcast.190), calls=%async_computation.3 | async-start | bytes 1048576 | tf_op jit(solution)/shard_map/all_to_all | solution.py:20
  104.9 18.7 %copy-start.4 = (f32[64,16]{0,1:T(8,128)S(1)}, f32[64,16]{0,1:T(8,128)}, u32[]{:S(2)}) copy-start(f32[64,16]{0,1:T(8,128)} %param.28) | copy-start | bytes 12292
  113.2 15.4 %copy-start.7 = (bf16[256,128]{1,0:T(8,128)(2,1)S(1)}, bf16[256,128]{1,0:T(8,128)(2,1)}, u32[]{:S(2)}) copy-start(bf16[256,128]{1,0:T(8,128)(2,1)} %param.23) | copy-start | bytes 196612
  144.8 21.8 %all-to-all-start.4 = ((f32[32,2,16,128]{3,2,1,0:T(8,128)}), f32[32,2,16,128]{3,2,1,0:T(8,128)S(1)}, u32[]{:S(2)}, u32[]{:S(2)}) async-start(f32[32,2,16,128]{3,2,1,0:T(8,128)} %bitcast.192), calls=%async_computation.4 | async-start | bytes 1048576 | tf_op jit(solution)/shard_map/all_to_all | solution.py:16
  153.4 16.2 %copy-start.1 = (f32[128,16,128]{2,1,0:T(8,128)}, f32[128,16,128]{2,1,0:T(8,128)S(1)}, u32[]{:S(2)}) copy-start(f32[128,16,128]{2,1,0:T(8,128)S(1)} %scatter_fusion.3) | copy-start | bytes 3145732
  169.6 0.8 copy-start.2
where the time goes:
time: 171 us; the launch traced here: 170 us
  matrix products  46.6 us (27%)
  blocking collectives  32.9 us (19%)
  waiting for transfers between devices  32.3 us (19%)
  other arithmetic  25.7 us (15%)
  local copies, waits for them, and re-layouts  19.5 us (11%)
  starting transfers between devices  12.5 us (7%)
    all_to_all x1, waiting for transfers between devices, send_blocks(): lax.all_to_all(outgoing, ('band', 'lon'), split_axis=0, concat_axis=0, ti...  19.1 us
    all_to_all x1, blocking collectives, send_back(): lax.all_to_all(outgoing, ('band', 'lon'), split_axis=0, concat_axis=0, ti...  18.6 us
    dot_general x2, matrix products, one_group(): jnp.einsum('hk,skb->shb', w_mid[level_index], hidden, preferred_element_t...  14.7 us
    all_to_all x1, blocking collectives, post_requests(): lax.all_to_all(wanted, ('band', 'lon'), split_axis=0, concat_axis=0, tile...  14.3 us
    dot_general x2, matrix products, one_group(): jnp.einsum('fh,shb->sfb', w_out, hidden, preferred_element_type=jnp.float32)  13.8 us
    all_to_all x1, waiting for transfers between devices, send_back(): lax.all_to_all(outgoing, ('band', 'lon'), split_axis=0, concat_axis=0, ti...  13.2 us
    scatter-add x2, other arithmetic, local(): jnp.zeros((atm_state.shape[0],) + back.shape[1:], jnp.float32).at[served]  11.2 us
    scatter-add x2, other arithmetic, local(): ocean_flux = jnp.zeros((ocean_state.shape[0],) + fluxes.shape[1:], jnp.fl...  11.2 us
  transfers between devices with their start and end apart: 3, of which 2 were waited for; matrix products, arithmetic and copies ran while one was open for 19% of the time, Pallas kernels for 0%

commit v1 on v0

v1 whole, which is shorter than its diff:
```python
import functools

import jax
import jax.numpy as jnp
from jax import lax
from jax.experimental import pallas as pl
from jax.experimental.pallas import tpu as pltpu
from jax.sharding import PartitionSpec as P

MESH = pl.DeviceIdType.MESH
BF = jnp.bfloat16
F32 = jnp.float32
GROUP = 4


def dot(a, b):
    return jnp.dot(a, b, preferred_element_type=F32)


def silu_half(u):
    return (u + u * jnp.tanh(u)).astype(BF)


def kernel(
    n, lon_n,
    meta, want, orows, atm, ocean, wet, remap, w_in, w_mid, b_cols, w_out, b_out, up_a, up_o,
    out_a, out_o,
    idx_send, idx_recv, idx_smem, blk_send, blk_recv,
    bk_send, bk_recv, fw_send, fw_recv, bk2_send, bk2_recv,
    hid, w_in_h, w_mid_h, fx, fo, xr, ocean_slot, m_a, a_t, m_o, g_t,
    local_sem, s_idx, r_idx, s_blk, r_blk, s_bk, r_bk, s_fw, r_fw, s_bk2, r_bk2,
):
    me = lax.axis_index("band") * lon_n + lax.axis_index("lon")
    slots = 2 * n
    cf = out_a.shape[0] // atm.shape[0]
    ablk = atm.shape[0]
    oblk = ocean.shape[0]
    cells = atm.shape[2]
    ch = atm.shape[1]

    def dev(t):
        return (t // lon_n, t % lon_n)

    def ahead(k):
        return (me + k) % n

    def behind(k):
        return (me + n - k) % n

    def copy_to(src, dst, s_sem, r_sem, q):
        return pltpu.make_async_remote_copy(
            src_ref=src.at[:, q], dst_ref=dst.at[:, me],
            send_sem=s_sem.at[q], recv_sem=r_sem.at[me],
            device_id=dev(q), device_id_type=MESH,
        )

    def arrival(src, dst, s_sem, r_sem, q):
        return pltpu.make_async_remote_copy(
            src_ref=src.at[:, q], dst_ref=dst.at[:, q],
            send_sem=s_sem.at[q], recv_sem=r_sem.at[q],
            device_id=dev(q), device_id_type=MESH,
        )

    def each(fn):
        @pl.loop(1, n)
        def _(k):
            fn(k)

    barrier = pltpu.get_barrier_semaphore()
    each(lambda k: pl.semaphore_signal(barrier, inc=1, device_id=dev(ahead(k)), device_id_type=MESH))

    lane = lax.broadcasted_iota(jnp.int32, (n, 128), 1)
    wanted = want[0]
    rows = jnp.where(lane == 0, wanted[:, 0:1], jnp.where(lane == 1, wanted[:, 1:2], 0))
    idx_send[0] = rows.reshape(n, 1, 128)
    idx_recv[0, pl.ds(me, 1)] = idx_send[0, pl.ds(me, 1)]
    pl.semaphore_wait(barrier, n - 1)

    each(lambda k: copy_to(idx_send, idx_recv, s_idx, r_idx, ahead(k)).start())

    w_in_h[...] = (w_in[...].astype(F32) * 0.5).astype(BF)
    for l in range(2):
        w_mid_h[l] = (w_mid[l].astype(F32) * 0.5).astype(BF)
    oc = orows[0]
    io = lax.broadcasted_iota(jnp.int32, (n, oblk), 1)
    g = jnp.concatenate([(oc[:, j : j + 1] == io).astype(F32) for j in range(2)], axis=0)
    g_t[...] = g.T.astype(BF)
    gb = g.astype(BF)
    m_o[...] = lax.dot_general(gb, gb, (((1,), (1,)), ((), ())), preferred_element_type=F32).astype(BF)

    each(lambda k: arrival(idx_send, idx_recv, s_idx, r_idx, behind(k)).wait_recv())
    to_smem = pltpu.make_async_copy(idx_recv, idx_smem, local_sem)
    to_smem.start()
    to_smem.wait()

    @pl.loop(1, n)
    def _(k):
        q = ahead(k)
        for j in range(2):
            blk_send[j, q] = atm[idx_smem[0, q, 0, j]]
        copy_to(blk_send, blk_recv, s_blk, r_blk, q).start()

    for j in range(2):
        blk_recv[j, me] = atm[idx_smem[0, me, 0, j]]

    got = idx_recv[0].reshape(n, 128)
    ia = lax.broadcasted_iota(jnp.int32, (n, ablk), 1)
    a = jnp.concatenate([(got[:, j : j + 1] == ia).astype(F32) for j in range(2)], axis=0)
    a_t[...] = a.T.astype(BF)
    ab = a.astype(BF)
    m_a[...] = lax.dot_general(ab, ab, (((1,), (1,)), ((), ())), preferred_element_type=F32).astype(BF)

    def network(b, second, back_send, back_recv, s_sem, r_sem):
        where = []
        for i in range(GROUP):
            k = b * GROUP + i
            q = behind(k)

            @pl.when(k > 0)
            def _():
                if second:
                    arrival(fw_send, fw_recv, s_fw, r_fw, q).wait_recv()
                else:
                    arrival(blk_send, blk_recv, s_blk, r_blk, q).wait_recv()

            for j in range(2):
                where.append((k, j, q, j * n + q))
        wet_rows = []
        for t, (k, j, q, s) in enumerate(where):
            cols = slice(t * cells, (t + 1) * cells)
            row = wet[pl.ds(meta[s], 1), :]
            wet_rows.append((row * meta[2 * slots + s]).astype(F32))
            block = blk_recv[j, q]
            sea = ocean[meta[s]]
            if second:
                fwd = fw_recv[j, q].astype(F32)
                block = (
                    block.astype(F32)
                    + jnp.dot(up_a[...], fwd, precision=lax.Precision.HIGHEST, preferred_element_type=F32)
                ).astype(BF)
                total = fo[pl.ds(pl.multiple_of(s * cf, cf), cf), :]
                sea = (
                    sea.astype(F32)
                    + row.astype(F32)
                    * jnp.dot(up_o[...], total, precision=lax.Precision.HIGHEST, preferred_element_type=F32)
                ).astype(BF)
            hid[0:ch, cols] = dot(block, remap[meta[slots + s]]).astype(BF)
            hid[ch:, cols] = sea
        h = silu_half(dot(w_in_h[...], hid[...]) + b_cols[:, 0:1])
        h = silu_half(dot(w_mid_h[0], h) + b_cols[:, 1:2])
        h = silu_half(dot(w_mid_h[1], h) + b_cols[:, 2:3])
        flux = dot(w_out[...], h) + b_out[...]
        flux = (flux * jnp.concatenate(wet_rows, axis=1)).astype(BF)
        for t, (k, j, q, s) in enumerate(where):
            one = flux[:, t * cells : (t + 1) * cells]
            fx[pl.ds(pl.multiple_of(s * cf, cf), cf), :] = one.astype(F32)
            back = lax.dot_general(
                one, remap[meta[slots + s]], (((1,), (1,)), ((), ())), preferred_element_type=F32
            )
            back_send[j, q] = back.astype(BF)
        for i in range(GROUP):
            k, j, q, s = where[2 * i]

            @pl.when(k > 0)
            def _():
                copy_to(back_send, back_recv, s_sem, r_sem, q).start()

    def collect(back_send, back_recv, s_sem, r_sem):
        for j in range(2):
            back_recv[j, me] = back_send[j, me]
        each(lambda k: arrival(back_send, back_recv, s_sem, r_sem, behind(k)).wait_recv())
        xr[...] = back_recv[...].reshape(slots * cf, cells).astype(F32)

    def gathered(matrix, src, dst, count):
        for f in range(cf):
            x = src[pl.ds(f, slots, stride=cf), :].astype(BF)
            dst[pl.ds(f, count, stride=cf), :] = dot(matrix[...], x)

    @pl.loop(0, n // GROUP)
    def _(b):
        network(b, False, bk_send, bk_recv, s_bk, r_bk)

    gathered(m_o, fx, fo, slots)
    collect(bk_send, bk_recv, s_bk, r_bk)
    gathered(m_a, xr, xr, slots)
    fw_send[...] = xr[...].reshape(2, n, cf, cells).astype(BF)
    each(lambda k: copy_to(fw_send, fw_recv, s_fw, r_fw, ahead(k)).start())
    for j in range(2):
        fw_recv[j, me] = fw_send[j, me]

    @pl.loop(0, n // GROUP)
    def _(b):
        network(b, True, bk2_send, bk2_recv, s_bk2, r_bk2)

    gathered(g_t, fx, out_o, oblk)
    collect(bk2_send, bk2_recv, s_bk2, r_bk2)
    gathered(a_t, xr, out_a, ablk)

    def finish(k):
        q = ahead(k)
        copy_to(idx_send, idx_recv, s_idx, r_idx, q).wait_send()
        copy_to(blk_send, blk_recv, s_blk, r_blk, q).wait_send()
        copy_to(bk_send, bk_recv, s_bk, r_bk, q).wait_send()
        copy_to(fw_send, fw_recv, s_fw, r_fw, q).wait_send()
        copy_to(bk2_send, bk2_recv, s_bk2, r_bk2, q).wait_send()

    each(finish)


def local(
    band_n, lon_n,
    atm_state, ocean_state, wet_mask, remap_tiles, intersection_atm, intersection_ocean,
    intersection_tile, peer_count, w_in, w_mid, b_hidden, w_out, b_out, up_atm, up_ocean,
):
    n = band_n * lon_n
    ablk, ch, cells = atm_state.shape
    oblk = ocean_state.shape[0]
    cf = w_out.shape[0]
    slots = 2 * n
    live = (jnp.arange(2, dtype=jnp.int32)[:, None] < peer_count[0][None, :]).astype(jnp.int32)
    meta = jnp.concatenate([intersection_ocean[0].T, intersection_tile[0].T, live], axis=0).reshape(-1)
    b_cols = (b_hidden * 0.5).T
    vm = pl.BlockSpec(memory_space=pltpu.VMEM)
    sm = pl.BlockSpec(memory_space=pltpu.SMEM)

    def flux_buffer():
        return pltpu.VMEM((2, n, cf, cells), BF)

    out_a, out_o = pl.pallas_call(
        functools.partial(kernel, n, lon_n),
        out_shape=(
            jax.ShapeDtypeStruct((ablk * cf, cells), F32),
            jax.ShapeDtypeStruct((oblk * cf, cells), F32),
        ),
        in_specs=[sm] + [vm] * 13,
        out_specs=(vm, vm),
        scratch_shapes=[
            pltpu.VMEM((1, n, 1, 128), jnp.int32),
            pltpu.VMEM((1, n, 1, 128), jnp.int32),
            pltpu.SMEM((1, n, 1, 128), jnp.int32),
            pltpu.VMEM((2, n, ch, cells), BF),
            pltpu.VMEM((2, n, ch, cells), BF),
            flux_buffer(), flux_buffer(), flux_buffer(), flux_buffer(), flux_buffer(), flux_buffer(),
            pltpu.VMEM((w_in.shape[1], 2 * GROUP * cells), BF),
            pltpu.VMEM(w_in.shape, BF),
            pltpu.VMEM(w_mid.shape, BF),
            pltpu.VMEM((slots * cf, cells), F32),
            pltpu.VMEM((slots * cf, cells), F32),
            pltpu.VMEM((slots * cf, cells), F32),
            pltpu.VMEM((8, 128), F32),
            pltpu.VMEM((slots, slots), BF),
            pltpu.VMEM((ablk, slots), BF),
            pltpu.VMEM((slots, slots), BF),
            pltpu.VMEM((oblk, slots), BF),
            pltpu.SemaphoreType.DMA,
        ] + [pltpu.SemaphoreType.DMA((n,))] * 10,
        compiler_params=pltpu.CompilerParams(
            collective_id=0, has_side_effects=True, vmem_limit_bytes=60 * 1024 * 1024
        ),
    )(
        meta, intersection_atm, intersection_ocean, atm_state, ocean_state, wet_mask, remap_tiles,
        w_in, w_mid, b_cols, w_out, b_out[:, None], up_atm, up_ocean,
    )
    return out_a.reshape(ablk, cf, cells), out_o.reshape(oblk, cf, cells)


def solution(mesh):
    b3 = P(("band", "lon"), None, None)
    b2 = P(("band", "lon"), None)
    placed = (b3, b3, b2, P(), b3, b3, b3, b2) + (P(),) * 7
    return jax.shard_map(
        functools.partial(local, mesh.shape["band"], mesh.shape["lon"]),
        mesh=mesh,
        in_specs=placed,
        out_specs=(b3, b3),
        check_vma=False,
    )
```

time: 171 us -> 90.5 us (0.53)
  Pallas kernels: 0 us -> 75 us
  matrix products: 46.6 us -> 0 us
  blocking collectives: 32.9 us -> 0 us
  waiting for transfers between devices: 32.3 us -> 0 us
  other arithmetic: 25.7 us -> 2.05 us
  starting transfers between devices: 12.5 us -> 0 us
  local copies, waits for them, and re-layouts: 19.5 us -> 12.4 us
    pallas_call x0 -> x1, Pallas kernels: none -> 75 us  [local(): pl.pallas_call(functools.partial(kernel, n, lon_n), out_shape=(jax.ShapeD...]
    dot_general x10 -> x0, matrix products: 46.6 us -> none  [the longest x2 14.7 us: one_group(): jnp.einsum('hk,skb->shb', w_mid[level_index], hidden, preferred_element_t...]
    all_to_all x2 -> x0, blocking collectives: 32.9 us -> none  [the longest x1 18.6 us: send_back(): lax.all_to_all(outgoing, ('band', 'lon'), split_axis=0, concat_axis=0, ti...]
    all_to_all x3 -> x0, waiting for transfers between devices: 32.3 us -> none  [the longest x1 19.1 us: send_blocks(): lax.all_to_all(outgoing, ('band', 'lon'), split_axis=0, concat_axis=0, ti...]
    scatter-add x4 -> x0, other arithmetic: 22.5 us -> none  [the longest x2 11.2 us: local(): jnp.zeros((atm_state.shape[0],) + back.shape[1:], jnp.float32).at[served]]
    gather x6 -> x0, local copies, waits for them, and re-layouts: 13.4 us -> none  [the longest x2 6.48 us: local(): ocean_now[ocean_rows]]
    all_to_all x3 -> x0, starting transfers between devices: 12.5 us -> none  [the longest x1 5.6 us: send_back(): lax.all_to_all(outgoing, ('band', 'lon'), split_axis=0, concat_axis=0, ti...]
    unnamed x22 -> x6, local copies, waits for them, and re-layouts: 2.36 us -> 9.62 us
  transfers between devices with their start and end apart: 3 -> 0, of which waited for: 2 -> 0; matrix products, arithmetic and copies ran while one was open for 19% -> 0% of each run, Pallas kernels for 0% -> 0%
where the time goes in v1:
time: 90.5 us; the launch traced here: 90.1 us
  Pallas kernels  75 us (83%)
  local copies, waits for them, and re-layouts  12.4 us (14%)
  other arithmetic  2.05 us (2%)
    pallas_call x1, Pallas kernels, local(): pl.pallas_call(functools.partial(kernel, n, lon_n), out_shape=(jax.ShapeD...  75 us
    unnamed x6, local copies, waits for them, and re-layouts  9.62 us

profile of v1, /device:TPU:0, one launch (start us, length us, event | category | flops | bytes accessed | tf_op | source)
XLA Modules:
  0.0 90.1 jit_solution(9048728681617493336)
XLA Ops:
  0.6 0.7 compare_convert_fusion
  1.3 0.7 pad_add_fusion
  2.0 0.6 reshape.13.meta
  2.6 0.7 broadcast_multiply_fusion
  3.3 1.3 %copy.27.b_out = f32[16,1]{1,0:T(8,128)} copy(f32[16,1]{0,1:T(1,128)} %bitcast.16) | data formatting | bytes 128 | tf_op jit(solution)/shard_map/broadcast_in_dim | solution.py:262
  4.7 1.4 %copy.25.want = s32[1,32,2]{2,1,0:T(8,128)} copy(s32[1,32,2]{1,2,0:T(2,128)} %param.19) | data formatting | bytes 512 | tf_op args[4]
  6.0 1.4 %copy.26.orows = s32[1,32,2]{2,1,0:T(8,128)} copy(s32[1,32,2]{1,2,0:T(2,128)} %param.20) | data formatting | bytes 512 | tf_op args[5]
  7.4 1.4 %copy.28.up_a = f32[64,16]{1,0:T(8,128)} copy(f32[64,16]{0,1:T(8,128)} %param.28) | data formatting | bytes 8192 | tf_op args[13]
  8.8 1.4 %copy.29.up_o = f32[64,16]{1,0:T(8,128)} copy(f32[64,16]{0,1:T(8,128)} %param.29) | data formatting | bytes 8192 | tf_op args[14]
  10.1 0.8 copy.24
  10.9 75.0 %shard_map.158 = (f32[1024,128]{1,0:T(8,128)}, f32[2048,128]{1,0:T(8,128)}) custom-call(s32[192]{0:T(256)} %reshape.13.meta, s32[1,32,2]{2,1,0:T(8,128)} %copy.25.want, s32[1,32,2]{2,1,0:T(8,128)} %copy.26.orows, bf16[64,64,128]{2,1,0:T(8,128)(2,1)} %atm.1, bf16[128,64,128]{2,1,0:T(8,128)(2,1)} %ocean.1, s32[128,128]{1,0:T(8,128)} %wet.1, ...), custom_call_target="tpu_custom_call" | custom-call | tf_op jit(solution)/shard_map/pallas_call | solution.py:229
  86.0 1.9 %copy.32 = f32[64,16,128]{2,1,0:T(8,128)} copy(f32[64,16,128]{2,1,0:T(8,128)} %bitcast.12) | data formatting | bytes 1048576
  87.8 2.3 %copy.33 = f32[128,16,128]{2,1,0:T(8,128)} copy(f32[128,16,128]{2,1,0:T(8,128)} %bitcast.11) | data formatting | bytes 2097152
